TPU v7x, 32 devices: a whole 2x2x4 slice. The times are simulated.
32 devices in a mesh: groups: 2 (over y), seq: 4 (over z), section: 4 (over x, core).
Axes of the slice: x: 2, y: 2, z: 4, core: 2. Of those that a mesh axis runs over, the one named last changes fastest.
Arguments:
- hidden: bfloat16 [4, 32, 3072], P('section', ('groups', 'seq')), parts along dimension 1, may hold values from -6 to 6
- kv_cache: bfloat16 [4, 4, 32, 2, 3072], P('section', None, ('groups', 'seq')), parts along dimension 2, may hold values from -400 to 400
- w_qkv: bfloat16 [4, 3072, 3, 3072], P('section', None, None, 'seq'), may hold values from -0.109375 to 0.109375
- w_out: bfloat16 [4, 3072, 3072], P('section', None, 'seq'), may hold values from -0.109375 to 0.109375
- norm_gain: float32 [4, 2, 128], P('section'), may hold values from 1 to 2
- modulation: float32 [4, 4, 3, 3072], P('section'), may hold values from -5 to 5
- patch_order: int32 [8], P('groups'), parts along dimension 0, may hold values from 0 to 3, each once
- timestep: int32 [8], P('groups'), parts along dimension 0, may hold values from 0 to 3
Outputs:
- next_hidden: bfloat16 [4, 32, 3072], P('section', ('groups', 'seq')), parts along dimension 1
- fresh_kv: bfloat16 [4, 32, 2, 3072], P('section', ('groups', 'seq')), parts along dimension 1
There are 2 independent parts, one for each index of `groups`. A program takes and returns all parts, laid end to end along the dimension named above; an argument that names none is the same for every part. Nothing has to cross between parts.
Inputs may be any that keep to these rules, and one draw needn't show every extreme that they name: `patch_order`: each section holds a different patch.
All inputs are finite; a program needn't handle non-finite values.
Results may differ from a plain program's by a relative error of at most 0.02.
The roundings to bfloat16 on the way count: a program that leaves them out, or rounds other values in their place, can miss the bound.
Values may be sent and summed in bfloat16 or wider, within the bound.
No kernel may reach another device: no remote copies, remote signals or barrier semaphores. Data moves between devices by JAX's collectives and lax.ppermute only.
A program may use at most 64 MiB of HBM per device.

v0:
```python
import math

import jax
import jax.numpy as jnp
from jax import lax
from jax.sharding import PartitionSpec as P


def passed_along(array, axis, by):
    count = lax.axis_size(axis)
    return lax.ppermute(array, axis, [(i, (i + by) % count) for i in range(count)])


def layer_norm(values_in):
    center = values_in - jnp.mean(values_in, axis=-1, keepdims=True)
    spread = jnp.mean(center * center, axis=-1, keepdims=True)
    return center * lax.rsqrt(spread + 1e-06)


def head_norm(values_in, gain):
    square = jnp.mean(values_in * values_in, axis=-1, keepdims=True)
    return values_in * lax.rsqrt(square + 1e-06) * gain


def body(hidden, kv_cache, w_qkv, w_out, norm_gain, modulation, patch_order, timestep):
    section_index = lax.axis_index("section")
    patch_index = lax.dynamic_index_in_dim(patch_order, section_index, 0, keepdims=False)
    step_index = lax.dynamic_index_in_dim(timestep, section_index, 0, keepdims=False)
    modulate = lax.dynamic_index_in_dim(modulation[0], step_index, 0, keepdims=False)
    model_width = hidden.shape[2]
    head_size = norm_gain.shape[2]
    head_count = model_width // head_size
    col_width = w_qkv.shape[3]
    rows_in = hidden[0].astype(jnp.float32)
    own_count = rows_in.shape[0]
    normed = (layer_norm(rows_in) * (1.0 + modulate[1]) + modulate[0]).astype(jnp.bfloat16)
    w_local = w_qkv[0].reshape(model_width, 3 * col_width)
    projected = jnp.dot(
        lax.all_gather(normed, "seq", axis=0, tiled=True),
        w_local,
        preferred_element_type=jnp.float32,
    ).astype(jnp.bfloat16)
    patch_len = projected.shape[0]
    projected = projected.reshape(patch_len, 3, col_width)
    query_cols = lax.all_gather(projected[:, 0], "seq", axis=1, tiled=True)
    kv_rows = lax.all_to_all(projected[:, 1:], "seq", split_axis=0, concat_axis=2, tiled=True)
    queries = head_norm(
        query_cols.astype(jnp.float32).reshape(patch_len, head_count, head_size), norm_gain[0, 0]
    ).astype(jnp.bfloat16)
    key_rows = head_norm(
        kv_rows[:, 0].astype(jnp.float32).reshape(own_count, head_count, head_size), norm_gain[0, 1]
    ).astype(jnp.bfloat16)
    fresh = jnp.stack([key_rows.reshape(own_count, model_width), kv_rows[:, 1]], axis=1)
    zero = jnp.zeros((), jnp.int32)
    local_kv = lax.dynamic_update_slice(kv_cache[0], fresh[None], (patch_index, zero, zero, zero))
    patch_count = local_kv.shape[0]
    local_keys = local_kv[:, :, 0].reshape(patch_count * own_count, head_count, head_size)
    local_values = local_kv[:, :, 1].reshape(patch_count * own_count, head_count, head_size)
    scores = jnp.einsum(
        "thd,shd->hts", queries, local_keys, preferred_element_type=jnp.float32
    ) / math.sqrt(head_size)
    row_top = lax.pmax(jnp.max(scores, axis=-1), "seq")
    weights = jnp.exp(scores - row_top[:, :, None]).astype(jnp.bfloat16)
    denominator = jnp.sum(weights, axis=-1, dtype=jnp.float32).T
    numerator = jnp.einsum(
        "hts,shd->thd", weights, local_values, preferred_element_type=jnp.float32
    ).reshape(patch_len, model_width)
    totals, counts = (
        lax.psum(numerator.astype(jnp.bfloat16), "seq").astype(jnp.float32),
        lax.psum(denominator.astype(jnp.bfloat16), "seq").astype(jnp.float32),
    )
    attention = (totals.reshape(patch_len, head_count, head_size) / counts[:, :, None]).astype(
        jnp.bfloat16
    )
    attention = attention.reshape(patch_len, model_width)
    out_cols = jnp.dot(attention, w_out[0], preferred_element_type=jnp.float32).astype(jnp.bfloat16)
    out_rows = lax.all_to_all(out_cols, "seq", split_axis=0, concat_axis=1, tiled=True)
    block = (rows_in + modulate[2] * out_rows.astype(jnp.float32)).astype(jnp.bfloat16)
    arrived = passed_along(block, "section", 1)
    return (arrived[None], fresh[None])


def solution(mesh):
    return jax.shard_map(
        body,
        mesh=mesh,
        in_specs=(
            P("section", ("groups", "seq"), None),
            P("section", None, ("groups", "seq"), None, None),
            P("section", None, None, "seq"),
            P("section", None, "seq"),
            P("section", None, None),
            P("section", None, None, None),
            P("groups"),
            P("groups"),
        ),
        out_specs=(
            P("section", ("groups", "seq"), None),
            P("section", ("groups", "seq"), None, None),
        ),
        check_vma=False,
    )
```

profile of v0, /device:TPU:0, one launch (start us, length us, event | category | flops | bytes accessed | tf_op | source)
XLA Modules:
  0.0 156.7 jit_solution(8221485039574207923)
XLA Ops:
  7.2 1.2 dynamic_slice.11
  9.7 0.9 convert_reduce_fusion
  10.6 0.9 fusion.15
  12.2 0.9 constant_dynamic-slice_fusion
  13.1 0.8 fusion.21
  13.9 15.1 %all-gather.1 = bf16[4,4,3072]{2,1,0:T(4,128)(2,1)S(1)} all-gather(bf16[1,4,3072]{2,1,0:T(4,128)(2,1)S(1)} %fusion.21), channel_id=1, replica_groups=mesh['groups'=2,'seq'=4,'section'=4] {'seq'}, dimensions={0}, use_global_device_ids=true | all-gather | bytes 122880 | tf_op jit(solution)/shard_map/all_gather | solution.py:39
  29.0 18.6 %copy.27 = bf16[1,3072,3,768]{1,3,2,0:T(8,128)(2,1)} copy(bf16[1,3072,3,768]{3,1,2,0:T(8,128)(2,1)} %param.10) | data formatting | bytes 28311552 | tf_op args[2]
  47.7 0.0 copy-start.2
  47.7 0.0 copy-start.3
  47.7 0.0 copy-start
  47.7 0.0 copy-start.1
  47.7 8.8 %convolution_convert_fusion = bf16[16,2304]{1,0:T(8,128)(2,1)S(1)} fusion(bf16[16,3072]{1,0:T(8,128)(2,1)S(1)} %reshape.88, bf16[3072,2304]{0,1:T(8,128)(2,1)} %bitcast.72), kind=kOutput, calls=%fused_computation.2 | convolution fusion | flops 226529280 | bytes 14327808 | tf_op jit(solution)/shard_map/dot_general | solution.py:38
  56.5 0.1 reshape.77
  56.6 0.7 slice.47
  57.2 4.7 %all-to-all-start = ((bf16[16,2,768]{2,1,0:T(2,128)(2,1)}), bf16[16,2,768]{2,1,0:T(2,128)(2,1)S(1)}, u32[]{:S(2)}, u32[]{:S(2)}) async-start(bf16[16,2,768]{2,1,0:T(2,128)(2,1)} %slice.47), calls=%async_computation | async-start | bytes 98304 | tf_op jit(solution)/shard_map/all_to_all | solution.py:46
  62.0 0.0 all-reduce.2.cloned.1.call-start
  62.0 14.3 %all-gather = bf16[16,1,3072]{2,1,0:T(2,128)(2,1)S(1)} all-gather(bf16[16,1,768]{2,1,0:T(2,128)(2,1)S(1)} %slice.51), channel_id=2, replica_groups=mesh['groups'=2,'seq'=4,'section'=4] {'seq'}, dimensions={2}, use_global_device_ids=true | all-gather | bytes 122880 | tf_op jit(solution)/shard_map/all_gather | solution.py:45
  76.3 0.2 reshape.84
  76.5 0.1 multiply_reduce_fusion
  76.6 0.0 copy-done.2
  76.6 0.1 multiply_convert_fusion
  76.8 0.0 copy-done.3
  76.8 0.6 dynamic_slice.13
  79.3 0.0 all-to-all-done
  79.4 0.1 slice.49
  79.5 0.1 reduce_sum.50
  79.6 0.1 mul.95
  79.7 0.1 multiply_convert_fusion.1
  79.7 0.0 copy-done
  79.8 0.8 constant_dynamic-update-slice_fusion
  80.5 0.9 slice_reduce_fusion.1
  81.4 0.2 fusion.23
  81.6 18.4 %pmax.7 = f32[24,16]{1,0:T(8,128)S(1)} all-reduce(f32[24,16]{1,0:T(8,128)S(1)} %get-tuple-element.11), channel_id=1, replica_groups=mesh['groups'=2,'seq'=4,'section'=4] {'seq'}, use_global_device_ids=true, to_apply=%region_5.6 | all-reduce | flops 384 | bytes 3072 | tf_op jit(solution)/shard_map/pmax | solution.py:62
  100.1 0.2 fusion.2
  100.3 0.6 copy.52
  101.0 0.0 all-reduce.2.cloned.1.call-update
  101.0 0.1 fusion.22
  101.1 0.1 copy.34
  101.2 8.3 %psum.15 = bf16[16,24]{1,0:T(8,128)(2,1)S(1)} all-reduce(bf16[16,24]{1,0:T(8,128)(2,1)S(1)} %bitcast.89), channel_id=1, replica_groups=mesh['groups'=2,'seq'=4,'section'=4] {'seq'}, use_global_device_ids=true, to_apply=%region_8.9 | all-reduce | flops 384 | bytes 1536 | tf_op jit(solution)/shard_map/psum | solution.py:70
  109.5 24.3 %all-reduce.2.cloned.1.call-done = bf16[16,3072]{1,0:T(8,128)(2,1)} async-done(((bf16[16,3072]{1,0:T(8,128)(2,1)}), bf16[16,3072]{1,0:T(8,128)(2,1)}) %all-reduce.2.cloned.1.call-update) | async-done | bytes 98320 | tf_op jit(solution)/shard_map/psum | solution.py:69
  133.8 0.1 div.43
  133.9 3.1 %fusion.3 = bf16[16,768]{1,0:T(8,128)(2,1)S(1)} fusion(bf16[1,3072,768]{2,1,0:T(8,128)(2,1)} %param.11, f32[2,8,24,128]{3,2,1,0:T(8,128)S(1)} %bitcast.76, bf16[16,3072]{1,0:T(8,128)(2,1)} %all-reduce.2.cloned.1.call-done), kind=kOutput, calls=%fused_computation.6 | convolution fusion | flops 75657216 | bytes 5038080 | tf_op jit(solution)/shard_map/dot_general | solution.py:76
  137.1 8.9 %all_to_all.31 = bf16[4,4,768]{2,1,0:T(4,128)(2,1)S(1)} all-to-all(bf16[4,4,768]{2,1,0:T(4,128)(2,1)S(1)} %all_to_all.27), channel_id=1, replica_groups=mesh['groups'=2,'seq'=4,'section'=4] {'seq'}, dimensions={0} | all-to-all | bytes 49152 | tf_op jit(solution)/shard_map/all_to_all | solution.py:77
  145.9 0.0 copy-done.1
  146.0 0.1 collective-permute-start
  146.0 3.2 %collective-permute-done = bf16[4,3072]{1,0:T(4,128)(2,1)S(1)} collective-permute-done((bf16[4,3072]{1,0:T(4,128)(2,1)S(1)}, bf16[4,3072]{1,0:T(4,128)(2,1)S(1)}, u32[]{:S(2)}, u32[]{:S(2)}) %collective-permute-start) | collective-permute-done | bytes 24608 | tf_op jit(solution)/shard_map/ppermute | solution.py:11
  149.3 0.6 copy.58
  (15 shorter events, 0.3 us)
Async XLA Ops:
  47.7 28.9 %copy-start.2 = (f32[1,2,128]{2,1,0:T(2,128)S(1)}, f32[1,2,128]{2,1,0:T(2,128)}, u32[]{:S(2)}) copy-start(f32[1,2,128]{2,1,0:T(2,128)} %param.12) | copy-start | bytes 3076
  47.7 29.1 %copy-start.3 = (s32[4]{0:T(128)S(1)}, s32[4]{0:T(128)}, u32[]{:S(2)}) copy-start(s32[4]{0:T(128)} %param.14) | copy-start | bytes 52
  47.7 32.1 %copy-start = (bf16[1,4,4,2,3072]{4,3,2,1,0:T(2,128)(2,1)S(1)}, bf16[1,4,4,2,3072]{4,3,2,1,0:T(2,128)(2,1)}, u32[]{:S(2)}) copy-start(bf16[1,4,4,2,3072]{4,3,2,1,0:T(2,128)(2,1)} %param.9) | copy-start | bytes 589828
  47.7 98.3 %copy-start.1 = (bf16[1,4,3072]{2,1,0:T(4,128)(2,1)S(1)}, bf16[1,4,3072]{2,1,0:T(4,128)(2,1)}, u32[]{:S(2)}) copy-start(bf16[1,4,3072]{2,1,0:T(4,128)(2,1)} %param.8) | copy-start | bytes 73732
  57.2 22.1 %all-to-all-start = ((bf16[16,2,768]{2,1,0:T(2,128)(2,1)}), bf16[16,2,768]{2,1,0:T(2,128)(2,1)S(1)}, u32[]{:S(2)}, u32[]{:S(2)}) async-start(bf16[16,2,768]{2,1,0:T(2,128)(2,1)} %slice.47), calls=%async_computation | async-start | bytes 98304 | tf_op jit(solution)/shard_map/all_to_all | solution.py:46
  62.0 71.9 %all-reduce.2.cloned.1.call-start = ((), (), s32[]{:S(2)}) async-start(), calls=%async_computation.2 | async-start | bytes 196608 | tf_op jit(solution)/shard_map/psum | solution.py:69
  146.0 3.3 %collective-permute-start = (bf16[4,3072]{1,0:T(4,128)(2,1)S(1)}, bf16[4,3072]{1,0:T(4,128)(2,1)S(1)}, u32[]{:S(2)}, u32[]{:S(2)}) collective-permute-start(bf16[4,3072]{1,0:T(4,128)(2,1)S(1)} %fusion.19), channel_id=1, source_target_pairs={{0,1},{1,2},{2,3},{3,0},{4,5},{5,6},{6,7},{7,4},{8,9},{9,10},{10,1... | collective-permute-start | bytes 73736 | tf_op jit(solution)/shard_map/ppermute | solution.py:11
Sparse Core Ops, SparseCore 0:
  101.1 32.6 all-reduce.1
where the time goes:
time: 158 us; the launch traced here: 157 us
  blocking collectives  65 us (41%)
  waiting for transfers between devices  27.6 us (17%)
  local copies, waits for them, and re-layouts  23.9 us (15%)
  between operations  18.1 us (11%)
  matrix products  12.4 us (8%)
  other arithmetic  5.08 us (3%)
  starting transfers between devices  4.78 us (3%)
    psum x1, waiting for transfers between devices, body(): lax.psum(numerator.astype(jnp.bfloat16), 'seq').astype(jnp.float32)  24.3 us
    unnamed x11, local copies, waits for them, and re-layouts  19.3 us
    pmax x1, blocking collectives, body(): row_top = lax.pmax(jnp.max(scores, axis=-1), 'seq')  18.4 us
    all_gather x1, blocking collectives, body(): lax.all_gather(normed, 'seq', axis=0, tiled=True)  15.1 us
    all_gather x1, blocking collectives, body(): query_cols = lax.all_gather(projected[:, 0], 'seq', axis=1, tiled=True)  14.3 us
    all_to_all x1, blocking collectives, body(): lax.all_to_all(out_cols, 'seq', split_axis=0, concat_axis=1, tiled=True)  8.86 us
    dot_general x1, matrix products, body(): jnp.dot(lax.all_gather(normed, 'seq', axis=0, tiled=True), w_local, prefe...  8.81 us
    psum x1, blocking collectives, body(): lax.psum(denominator.astype(jnp.bfloat16), 'seq').astype(jnp.float32)  8.35 us
  transfers between devices with their start and end apart: 3, of which 2 were waited for; matrix products, arithmetic and copies ran while one was open for 1% of the time, Pallas kernels for 0%

commit v1 on v0

--- a/solution.py
+++ b/solution.py
@@ -1,9 +1,20 @@
+import functools
 import math
 
 import jax
 import jax.numpy as jnp
 from jax import lax
+from jax.experimental import pallas as pl
+from jax.experimental.pallas import tpu as pltpu
 from jax.sharding import PartitionSpec as P
+
+
+APART = (1, 2)
+
+F32 = jnp.float32
+BF16 = jnp.bfloat16
+VMEM = pl.BlockSpec(memory_space=pltpu.VMEM)
+SMEM = pl.BlockSpec(memory_space=pltpu.SMEM)
 
 
 def passed_along(array, axis, by):
@@ -22,7 +33,249 @@
     return values_in * lax.rsqrt(square + 1e-06) * gain
 
 
-def body(hidden, kv_cache, w_qkv, w_out, norm_gain, modulation, patch_order, timestep):
+def swapped(slots, number):
+    return jnp.concatenate([slots[b ^ number] for b in range(len(slots))], axis=0)
+
+
+def ahead_kernel(out_ref):
+    out_ref[...] = jnp.zeros_like(out_ref)
+
+
+def pack_kernel(order_ref, _, hidden_ref, cache_ref, *outs, slots, patches, columns, split):
+    mine = lax.axis_index("seq")
+    patch = order_ref[lax.axis_index("section")]
+    hidden = hidden_ref[...].astype(F32)
+    hidden = [hidden[:, c * columns : (c + 1) * columns] for c in range(slots)]
+    hidden = jnp.concatenate(hidden, axis=0).astype(BF16)
+    for b in range(slots):
+        start = pl.multiple_of((mine ^ b) * columns, columns)
+        both = [
+            cache_ref[0, lax.rem(patch + i, patches), :, :, pl.ds(start, columns)].astype(F32)
+            for i in range(1, patches)
+        ]
+        both = jnp.concatenate(both, axis=0)
+        both = jnp.concatenate([both[:, 0], both[:, 1]], axis=0).astype(BF16)
+        outs[b][: both.shape[0]] = both
+        if b and b not in split:
+            outs[b][both.shape[0] :] = hidden
+
+
+def project_kernel(step_ref, mod_ref, gain_ref, weight_ref, *refs, slots, tokens, heads, size, stale):
+    hidden_refs = refs[:slots][::-1]
+    q_ref, held_ref, gate_ref = refs[slots : slots + 3]
+    fresh_refs, scratch = refs[slots + 3 : 2 * slots + 3], refs[2 * slots + 3]
+    mine = lax.axis_index("seq")
+    step = step_ref[lax.axis_index("section")]
+    columns = heads * size
+    shift = mod_ref[0, pl.ds(step, 1), :]
+    scale = mod_ref[1, pl.ds(step, 1), :]
+    start = pl.multiple_of(mine * columns, columns)
+    gate_ref[...] = mod_ref[2, pl.ds(step, 1), pl.ds(start, columns)]
+    rows = []
+    for ref in hidden_refs:
+        if ref.shape[0] == tokens:
+            rows.append(ref[...].astype(F32))
+        else:
+            cut = ref[2 * stale :].astype(F32)
+            rows.append(jnp.concatenate([cut[c * tokens : (c + 1) * tokens] for c in range(slots)], axis=1))
+    rows = jnp.concatenate(rows, axis=0)
+    scratch[...] = rows
+    normed = (layer_norm(rows) * (1.0 + scale) + shift).astype(BF16)
+    parts = []
+    for part in range(3):
+        dotted = jnp.dot(normed, weight_ref[part], preferred_element_type=F32)
+        parts.append(dotted.astype(BF16).astype(F32))
+    normed_heads = []
+    for part in range(2):
+        gain = gain_ref[pl.ds(part, 1), :]
+        normed_heads.append(
+            jnp.concatenate(
+                [head_norm(parts[part][:, h * size : (h + 1) * size], gain) for h in range(heads)], axis=1
+            )
+        )
+    q_ref[...] = normed_heads[0].astype(BF16)
+    keys, values = normed_heads[1], parts[2]
+    for b in range(slots):
+        own = slice(b * tokens, (b + 1) * tokens)
+        fresh_refs[b][...] = jnp.concatenate([keys[own], values[own]], axis=0).astype(BF16)
+    held_ref[...] = scratch[:, pl.ds(start, columns)].astype(BF16)
+
+
+def attend_kernel(q_ref, *refs, slots, tokens, stale, heads, size):
+    fresh_refs, old = refs[:slots], refs[slots : 2 * slots][::-1]
+    outs = refs[2 * slots : 3 * slots]
+    per = stale + tokens
+    fresh = [r[...].astype(F32) for r in fresh_refs]
+    old = [r[: 2 * stale].astype(F32) for r in old]
+    keys = jnp.concatenate([x for b in range(slots) for x in (old[b][:stale], fresh[b][:tokens])], axis=0).astype(BF16)
+    values = jnp.concatenate([x for b in range(slots) for x in (old[b][stale:], fresh[b][tokens:])], axis=0).astype(BF16)
+    count = slots * per
+    queries = q_ref[...]
+    length = queries.shape[0]
+    cuts = [slice(h * size, (h + 1) * size) for h in range(heads)]
+    dims = (((1,), (1,)), ((), ()))
+    scores = [lax.dot_general(queries[:, cut], keys[:, cut], dims, preferred_element_type=F32) for cut in cuts]
+    scores = jnp.concatenate(scores, axis=0) / math.sqrt(size)
+    top = jnp.max(scores, axis=-1, keepdims=True)
+    weights = jnp.exp(scores - top).astype(BF16).astype(F32)
+    lane = lax.broadcasted_iota(jnp.int32, weights.shape, 1)
+    apart = [jnp.where((lane >= b * per) & (lane < (b + 1) * per), weights, 0.0).astype(BF16) for b in range(slots)]
+    ones = jnp.ones((count, size), BF16)
+    sums = []
+    for h, cut in enumerate(cuts):
+        rows = jnp.concatenate([x[h * length : (h + 1) * length] for x in apart], axis=0)
+        extended = jnp.concatenate([values[:, cut], ones], axis=1)
+        sums.append(jnp.dot(rows, extended, preferred_element_type=F32))
+    rows = []
+    for both in sums:
+        both = both.astype(BF16).astype(F32)
+        total = both[:length]
+        for b in range(1, slots):
+            total = total + both[b * length : (b + 1) * length]
+        rows.append(total[:, :size] / total[:, size:])
+    rows = jnp.concatenate(rows, axis=1)
+    pieces = [rows[b * tokens : (b + 1) * tokens] for b in range(slots)]
+    for b in range(slots):
+        outs[b][:length] = swapped(pieces, b).astype(BF16)
+        outs[b][length:] = fresh_refs[b][...]
+
+
+def output_kernel(gate_ref, held_ref, weight_ref, *refs, slots, tokens):
+    columns = weight_ref.shape[1]
+    attention = refs[:slots][::-1]
+    mine = lax.axis_index("seq")
+    total = None
+    for b in range(slots):
+        start = pl.multiple_of((mine ^ b) * columns, columns)
+        term = jnp.dot(attention[b][: slots * tokens], weight_ref[pl.ds(start, columns), :], preferred_element_type=F32)
+        total = term if total is None else total + term
+    block = held_ref[...].astype(F32) + gate_ref[...] * total.astype(BF16).astype(F32)
+    for b in range(slots):
+        refs[slots + b][...] = block[b * tokens : (b + 1) * tokens].astype(BF16)
+
+
+def place_kernel(*refs, slots):
+    out_ref, refs = refs[slots], refs[:slots][::-1]
+    columns = refs[0].shape[1]
+    mine = lax.axis_index("seq")
+    for b in range(slots):
+        start = pl.multiple_of((mine ^ b) * columns, columns)
+        out_ref[0, :, pl.ds(start, columns)] = refs[b][...]
+
+
+def place_kv_kernel(*refs, slots, tokens):
+    out_ref, refs = refs[slots], refs[:slots][::-1]
+    columns = refs[0].shape[1]
+    mine = lax.axis_index("seq")
+    for b in range(slots):
+        start = pl.multiple_of((mine ^ b) * columns, columns)
+        piece = refs[b][slots * tokens :].astype(F32)
+        both = jnp.stack([piece[:tokens], piece[tokens:]], axis=1)
+        out_ref[0, :, :, pl.ds(start, columns)] = both.astype(BF16)
+
+
+def call(kernel, flops, out_shape, specs, operands, scratch=(), **sizes):
+    return pl.pallas_call(
+        functools.partial(kernel, **sizes),
+        out_shape=out_shape,
+        in_specs=specs + [VMEM] * (len(operands) - len(specs)),
+        out_specs=jax.tree.map(lambda _: VMEM, out_shape),
+        scratch_shapes=scratch,
+        compiler_params=pltpu.CompilerParams(vmem_limit_bytes=16 * 2**20),
+        cost_estimate=pl.CostEstimate(flops=int(flops), transcendentals=0, bytes_accessed=2**20),
+    )(*operands)
+
+
+def apart(slots):
+    return APART if slots > 2 else ()
+
+
+def body_by_heads(hidden, kv_cache, w_qkv, w_out, norm_gain, modulation, patch_order, timestep):
+    slots, sections = lax.axis_size("seq"), lax.axis_size("section")
+    tokens, width = hidden.shape[1:]
+    patches = kv_cache.shape[1]
+    columns, size = w_qkv.shape[3], norm_gain.shape[2]
+    heads, stale, rows = columns // size, (patches - 1) * tokens, slots * tokens
+    split = apart(slots)
+
+    def array(*shape, dtype=BF16):
+        return jax.ShapeDtypeStruct(shape, dtype)
+
+    def moved(array, number, onward=0):
+        pairs = [
+            (j * sections + s, (j ^ number) * sections + (s + onward) % sections)
+            for j in range(slots)
+            for s in range(sections)
+        ]
+        return lax.ppermute(array, ("seq", "section"), pairs)
+
+    def exchanged(arrays):
+        return [arrays[0]] + [moved(arrays[b], b) for b in range(1, slots)]
+
+    own = hidden[0]
+    alone = {b: moved(own, b) for b in split}
+    ahead = call(ahead_kernel, 5e9, array(8, 128, dtype=F32), [], [])
+    packed = call(
+        pack_kernel,
+        5e9,
+        [array(2 * stale + (rows if b and b not in split else 0), columns) for b in range(slots)],
+        [SMEM],
+        [patch_order, ahead, own, kv_cache],
+        slots=slots,
+        patches=patches,
+        columns=columns,
+        split=split,
+    )
+    old = exchanged(packed)
+    inputs = [own] + [alone[b] if b in split else old[b] for b in range(1, slots)]
+    queries, held, gate, *fresh = call(
+        project_kernel,
+        2e9,
+        [array(rows, columns), array(rows, columns), array(1, columns, dtype=F32)] + [array(2 * tokens, columns)] * slots,
+        [SMEM],
+        [
+            timestep,
+            jnp.transpose(modulation[0], (1, 0, 2)),
+            norm_gain[0],
+            jnp.transpose(w_qkv[0], (1, 0, 2)),
+            *inputs[::-1],
+        ],
+        scratch=[pltpu.VMEM((rows, width), F32)],
+        slots=slots,
+        tokens=tokens,
+        heads=heads,
+        size=size,
+        stale=stale,
+    )
+    ordered = call(
+        attend_kernel,
+        2e9,
+        [array(rows + 2 * tokens, columns)] * slots,
+        [],
+        [queries, *fresh, *old[::-1]],
+        slots=slots,
+        tokens=tokens,
+        stale=stale,
+        heads=heads,
+        size=size,
+    )
+    attention = exchanged(ordered)
+    pieces = call(
+        output_kernel,
+        2e9,
+        [array(tokens, columns)] * slots,
+        [],
+        [gate, held, w_out[0], *attention[::-1]],
+        slots=slots,
+        tokens=tokens,
+    )
+    arrived = [moved(pieces[b], b, onward=1) for b in range(slots)]
+    fresh_kv = call(place_kv_kernel, 1e9, array(1, tokens, 2, width), [], attention[::-1], slots=slots, tokens=tokens)
+    next_hidden = call(place_kernel, 1e9, array(1, tokens, width), [], arrived[::-1], slots=slots)
+    return (next_hidden, fresh_kv)
+
+
+def body_by_tokens(hidden, kv_cache, w_qkv, w_out, norm_gain, modulation, patch_order, timestep):
     section_index = lax.axis_index("section")
     patch_index = lax.dynamic_index_in_dim(patch_order, section_index, 0, keepdims=False)
     step_index = lax.dynamic_index_in_dim(timestep, section_index, 0, keepdims=False)
@@ -80,6 +333,13 @@
     return (arrived[None], fresh[None])
 
 
+def body(hidden, kv_cache, w_qkv, w_out, norm_gain, modulation, patch_order, timestep):
+    count = lax.axis_size("seq")
+    whole_heads = w_qkv.shape[3] % norm_gain.shape[2] == 0
+    chosen = body_by_heads if whole_heads and count & (count - 1) == 0 else body_by_tokens
+    return chosen(hidden, kv_cache, w_qkv, w_out, norm_gain, modulation, patch_order, timestep)
+
+
 def solution(mesh):
     return jax.shard_map(
         body,

time: 158 us -> 31.9 us (0.20)
  blocking collectives: 65 us -> 0 us
  waiting for transfers between devices: 27.6 us -> 4.38 us
  local copies, waits for them, and re-layouts: 23.9 us -> 0.92 us
  between operations: 18.1 us -> 0.85 us
  starting transfers between devices: 4.78 us -> 19.7 us
  matrix products: 12.4 us -> 0 us
  Pallas kernels: 0 us -> 5.84 us
  other arithmetic: 5.08 us -> 0.01 us
    all_gather x2 -> x0, blocking collectives: 29.3 us -> none  [the longest x1 15.1 us: body(): lax.all_gather(normed, 'seq', axis=0, tiled=True)]
    psum x1 -> x0, waiting for transfers between devices: 24.3 us -> none  [body(): lax.psum(numerator.astype(jnp.bfloat16), 'seq').astype(jnp.float32)]
    ppermute x1 -> x12, starting transfers between devices: 0.06 us -> 19.7 us  [moved(): return lax.ppermute(array, ('seq', 'section'), pairs)]
    pmax x1 -> x0, blocking collectives: 18.4 us -> none  [body(): row_top = lax.pmax(jnp.max(scores, axis=-1), 'seq')]
    unnamed x11 -> x24, local copies, waits for them, and re-layouts: 19.3 us -> 0.92 us
    dot_general x4 -> x0, matrix products: 12.4 us -> none  [the longest x1 8.81 us: body(): jnp.dot(lax.all_gather(normed, 'seq', axis=0, tiled=True), w_local, prefe...]
    all_to_all x1 -> x0, blocking collectives: 8.86 us -> none  [body(): lax.all_to_all(out_cols, 'seq', split_axis=0, concat_axis=1, tiled=True)]
    psum x1 -> x0, blocking collectives: 8.35 us -> none  [body(): lax.psum(denominator.astype(jnp.bfloat16), 'seq').astype(jnp.float32)]
  transfers between devices with their start and end apart: 3 -> 12, of which waited for: 2 -> 4; matrix products, arithmetic and copies ran while one was open for 1% -> 0% of each run, Pallas kernels for 0% -> 11%
where the time goes in v1:
time: 31.9 us; the launch traced here: 31.7 us
  starting transfers between devices  19.7 us (62%)
  Pallas kernels  5.84 us (18%)
  waiting for transfers between devices  4.38 us (14%)
  local copies, waits for them, and re-layouts  0.92 us (3%)
  between operations  0.85 us (3%)
    ppermute x12, starting transfers between devices, moved(): return lax.ppermute(array, ('seq', 'section'), pairs)  19.7 us
    pallas_call x7, Pallas kernels, call(): pl.pallas_call(functools.partial(kernel, **sizes), out_shape=out_shape, i...  5.84 us
    ppermute x12, waiting for transfers between devices, moved(): return lax.ppermute(array, ('seq', 'section'), pairs)  4.38 us
    unnamed x24, local copies, waits for them, and re-layouts  0.92 us
  transfers between devices with their start and end apart: 12, of which 4 were waited for; matrix products, arithmetic and copies ran while one was open for 0% of the time, Pallas kernels for 11%

profile of v1, /device:TPU:0, one launch (start us, length us, event | category | flops | bytes accessed | tf_op | source)
XLA Modules:
  0.0 31.7 jit_solution(9411031675499080262)
XLA Ops:
  0.6 0.0 copy-start.5
  0.6 0.0 copy-start.1
  0.7 0.0 copy-start.4
  0.7 0.0 copy-start.3
  0.7 0.0 copy-start
  0.7 0.0 copy-start.2
  0.7 0.0 slice-start
  0.7 0.0 slice-start.1
  0.7 0.6 %copy-done.5 = s32[4]{0:T(128)S(1)} copy-done((s32[4]{0:T(128)S(1)}, s32[4]{0:T(128)}, u32[]{:S(2)}) %copy-start.5) | copy-done | bytes 40
  1.3 0.1 copy-done.1
  1.4 0.2 copy-done.4
  1.6 0.7 %shard_map.96 = (bf16[24,768]{1,0:T(8,128)(2,1)S(1)}, bf16[24,768]{1,0:T(8,128)(2,1)S(1)}, bf16[24,768]{1,0:T(8,128)(2,1)S(1)}, bf16[40,768]{1,0:T(8,128)(2,1)S(1)}) custom-call(s32[4]{0:T(128)S(1)} %copy-done.5, f32[8,128]{1,0:T(8,128)S(1)} %shard_map.95._, bf16[4,3072]{1,0:T(4,128)(2,1)S(1)} %bitcast.13, bf16[1,4,4,2,3072]{4,3,2,1,0:T(2,128)(2,1)S(1)} %copy-done.4), custom_call_target="tpu_custom_call" | custom-call | flops 5000000000 | bytes 1048576 | tf_op jit(solution)/shard_map/pallas_call | solution.py:178
  2.3 0.0 slice-start.4
  2.3 5.1 %collective-permute-start = (bf16[40,768]{1,0:T(8,128)(2,1)S(1)}, bf16[40,768]{1,0:T(8,128)(2,1)S(1)}, u32[]{:S(2)}, u32[]{:S(2)}) collective-permute-start(bf16[40,768]{1,0:T(8,128)(2,1)S(1)} %get-tuple-element.21), channel_id=1, source_target_pairs={{0,12},{1,13},{2,14},{3,15},{4,8},{5,9},{6,10},{7,11},{8,4},{9,5},... | collective-permute-start | bytes 184328 | tf_op jit(solution)/shard_map/ppermute | solution.py:210
  7.4 0.0 collective-permute-start.1
  7.4 0.6 %collective-permute-start.2 = (bf16[4,3072]{1,0:T(4,128)(2,1)S(1)}, bf16[4,3072]{1,0:T(4,128)(2,1)S(1)}, u32[]{:S(2)}, u32[]{:S(2)}) collective-permute-start(bf16[4,3072]{1,0:T(4,128)(2,1)S(1)} %bitcast.15), channel_id=1, source_target_pairs={{0,4},{1,5},{2,6},{3,7},{4,0},{5,1},{6,2},{7,3},{8,12},{9,13},{10,... | collective-permute-start | bytes 73736 | tf_op jit(solution)/shard_map/ppermute | solution.py:210
  8.1 2.3 %collective-permute-start.3 = (bf16[24,768]{1,0:T(8,128)(2,1)S(1)}, bf16[24,768]{1,0:T(8,128)(2,1)S(1)}, u32[]{:S(2)}, u32[]{:S(2)}) collective-permute-start(bf16[24,768]{1,0:T(8,128)(2,1)S(1)} %get-tuple-element.29), channel_id=1, source_target_pairs={{0,8},{1,9},{2,10},{3,11},{4,12},{5,13},{6,14},{7,15},{8,0},{9,1},... | collective-permute-start | bytes 110600 | tf_op jit(solution)/shard_map/ppermute | solution.py:210
  10.4 2.0 %collective-permute-start.4 = (bf16[24,768]{1,0:T(8,128)(2,1)S(1)}, bf16[24,768]{1,0:T(8,128)(2,1)S(1)}, u32[]{:S(2)}, u32[]{:S(2)}) collective-permute-start(bf16[24,768]{1,0:T(8,128)(2,1)S(1)} %get-tuple-element.30), channel_id=1, source_target_pairs={{0,4},{1,5},{2,6},{3,7},{4,0},{5,1},{6,2},{7,3},{8,12},{9,13},{10,... | collective-permute-start | bytes 110600 | tf_op jit(solution)/shard_map/ppermute | solution.py:210
  12.4 0.2 collective-permute-done.1.refs_1_
  12.6 0.0 collective-permute-done.2.refs_2_
  12.6 0.0 collective-permute-done.refs_0_.refs_4_
  12.6 0.0 copy-done.3
  12.6 0.0 copy-done
  12.6 0.0 copy-done.2
  12.6 0.0 slice-done
  12.6 0.0 slice-done.1
  12.6 0.0 slice-start.5
  12.6 2.7 %shard_map.97 = (bf16[16,768]{1,0:T(8,128)(2,1)S(1)}, bf16[16,768]{1,0:T(8,128)(2,1)S(1)}, f32[1,768]{1,0:T(1,128)S(1)}, bf16[8,768]{1,0:T(8,128)(2,1)S(1)}, bf1...) custom-call(s32[4]{0:T(128)S(1)} %copy-done.3, f32[3,4,3072]{2,1,0:T(4,128)S(1)} %bitcast.12, ...), custom_call_target="tpu_custom_call" | custom-call | flops 2000000000 | bytes 1048576 | tf_op jit(solution)/shard_map/pallas_call | solution.py:178
  15.3 0.0 collective-permute-done.3.refs_5_
  15.3 0.0 collective-permute-done.4.refs_6_
  15.4 0.4 %shard_map.98 = (bf16[24,768]{1,0:T(8,128)(2,1)S(1)}, bf16[24,768]{1,0:T(8,128)(2,1)S(1)}, bf16[24,768]{1,0:T(8,128)(2,1)S(1)}, bf16[24,768]{1,0:T(8,128)(2,1)S(1)}) custom-call(bf16[16,768]{1,0:T(8,128)(2,1)S(1)} %get-tuple-element.24.q_ref, bf16[8,768]{1,0:T(8,128)(2,1)S(1)} %get-tuple-element.25.refs_0_, bf16[8,768]{1,0:T(8,128)(2,1)S(1)} %get-tuple-element.26.refs_1_, ...), custom_call_target="tpu_custom_call" | custom-call | flops 2000000000 | bytes 1048576 | tf_op jit(solution)/shard_map/pallas_call | solution.py:178
  15.8 1.6 %collective-permute-start.5 = (bf16[24,768]{1,0:T(8,128)(2,1)S(1)}, bf16[24,768]{1,0:T(8,128)(2,1)S(1)}, u32[]{:S(2)}, u32[]{:S(2)}) collective-permute-start(bf16[24,768]{1,0:T(8,128)(2,1)S(1)} %get-tuple-element.32), channel_id=1, source_target_pairs={{0,12},{1,13},{2,14},{3,15},{4,8},{5,9},{6,10},{7,11},{8,4},{9,5},... | collective-permute-start | bytes 110600 | tf_op jit(solution)/shard_map/ppermute | solution.py:210
  17.4 0.9 %collective-permute-start.6 = (bf16[24,768]{1,0:T(8,128)(2,1)S(1)}, bf16[24,768]{1,0:T(8,128)(2,1)S(1)}, u32[]{:S(2)}, u32[]{:S(2)}) collective-permute-start(bf16[24,768]{1,0:T(8,128)(2,1)S(1)} %get-tuple-element.33), channel_id=1, source_target_pairs={{0,8},{1,9},{2,10},{3,11},{4,12},{5,13},{6,14},{7,15},{8,0},{9,1},... | collective-permute-start | bytes 110600 | tf_op jit(solution)/shard_map/ppermute | solution.py:210
  18.3 1.9 %collective-permute-start.7 = (bf16[24,768]{1,0:T(8,128)(2,1)S(1)}, bf16[24,768]{1,0:T(8,128)(2,1)S(1)}, u32[]{:S(2)}, u32[]{:S(2)}) collective-permute-start(bf16[24,768]{1,0:T(8,128)(2,1)S(1)} %get-tuple-element.34), channel_id=1, source_target_pairs={{0,4},{1,5},{2,6},{3,7},{4,0},{5,1},{6,2},{7,3},{8,12},{9,13},{10,... | collective-permute-start | bytes 110600 | tf_op jit(solution)/shard_map/ppermute | solution.py:210
  20.2 1.4 %collective-permute-done.5.refs_0_ = bf16[24,768]{1,0:T(8,128)(2,1)S(1)} collective-permute-done((bf16[24,768]{1,0:T(8,128)(2,1)S(1)}, bf16[24,768]{1,0:T(8,128)(2,1)S(1)}, u32[]{:S(2)}, u32[]{:S(2)}) %collective-permute-start.5) | collective-permute-done | bytes 36896 | tf_op jit(solution)/shard_map/ppermute | solution.py:210
  21.6 1.1 %collective-permute-done.6.refs_1_ = bf16[24,768]{1,0:T(8,128)(2,1)S(1)} collective-permute-done((bf16[24,768]{1,0:T(8,128)(2,1)S(1)}, bf16[24,768]{1,0:T(8,128)(2,1)S(1)}, u32[]{:S(2)}, u32[]{:S(2)}) %collective-permute-start.6) | collective-permute-done | bytes 36896 | tf_op jit(solution)/shard_map/ppermute | solution.py:210
  22.7 0.0 collective-permute-done.7.refs_2_
  22.7 0.7 %shard_map.99 = (bf16[4,768]{1,0:T(4,128)(2,1)S(1)}, bf16[4,768]{1,0:T(4,128)(2,1)S(1)}, bf16[4,768]{1,0:T(4,128)(2,1)S(1)}, bf16[4,768]{1,0:T(4,128)(2,1)S(1)}) custom-call(f32[1,768]{1,0:T(1,128)S(1)} %get-tuple-element.22.gate_ref, bf16[16,768]{1,0:T(8,128)(2,1)S(1)} %get-tuple-element.23.held_ref, bf16[3072,768]{1,0:T(8,128)(2,1)S(1)} %bitcast.20, ...), custom_call_target="tpu_custom_call" | custom-call | flops 2000000000 | bytes 1048576 | tf_op jit(solution)/shard_map/pallas_call | solution.py:178
  23.4 0.1 collective-permute-start.8
  23.5 3.6 %collective-permute-start.9 = (bf16[4,768]{1,0:T(4,128)(2,1)S(1)}, bf16[4,768]{1,0:T(4,128)(2,1)S(1)}, u32[]{:S(2)}, u32[]{:S(2)}) collective-permute-start(bf16[4,768]{1,0:T(4,128)(2,1)S(1)} %get-tuple-element.37), channel_id=1, source_target_pairs={{0,9},{1,10},{2,11},{3,8},{4,13},{5,14},{6,15},{7,12},{8,1},{9,2},... | collective-permute-start | bytes 18440 | tf_op jit(solution)/shard_map/ppermute | solution.py:210
  27.1 0.0 collective-permute-start.10
  27.1 1.5 %collective-permute-start.11 = (bf16[4,768]{1,0:T(4,128)(2,1)S(1)}, bf16[4,768]{1,0:T(4,128)(2,1)S(1)}, u32[]{:S(2)}, u32[]{:S(2)}) collective-permute-start(bf16[4,768]{1,0:T(4,128)(2,1)S(1)} %get-tuple-element.39), channel_id=1, source_target_pairs={{0,1},{1,2},{2,3},{3,0},{4,5},{5,6},{6,7},{7,4},{8,9},{9,10},{10,1... | collective-permute-start | bytes 18440 | tf_op jit(solution)/shard_map/ppermute | solution.py:210
  28.6 0.7 %shard_map.101 = bf16[1,4,2,3072]{3,2,1,0:T(2,128)(2,1)} custom-call(bf16[24,768]{1,0:T(8,128)(2,1)S(1)} %collective-permute-done.5.refs_0_, bf16[24,768]{1,0:T(8,128)(2,1)S(1)} %collective-permute-done.6.refs_1_, bf16[24,768]{1,0:T(8,128)(2,1)S(1)} %collective-permute-done.7.refs_2_, bf16[24,768]{1,0:T(8,128)(2,1)S(1)} %get-tuple-element.35.refs_3_), custom_call_target="tpu_custom_call" | custom-call | flops 1000000000 | bytes 1048576 | tf_op jit(solution)/shard_map/pallas_call | solution.py:178
  29.3 0.0 collective-permute-done.8.refs_0_
  29.3 0.0 collective-permute-done.9.refs_1_
  29.3 1.8 %collective-permute-done.10.refs_2_ = bf16[4,768]{1,0:T(4,128)(2,1)S(1)} collective-permute-done((bf16[4,768]{1,0:T(4,128)(2,1)S(1)}, bf16[4,768]{1,0:T(4,128)(2,1)S(1)}, u32[]{:S(2)}, u32[]{:S(2)}) %collective-permute-start.10) | collective-permute-done | bytes 6176 | tf_op jit(solution)/shard_map/ppermute | solution.py:210
  31.1 0.0 collective-permute-done.11.refs_3_
  31.1 0.6 %shard_map.100 = bf16[1,4,3072]{2,1,0:T(4,128)(2,1)} custom-call(bf16[4,768]{1,0:T(4,128)(2,1)S(1)} %collective-permute-done.8.refs_0_, bf16[4,768]{1,0:T(4,128)(2,1)S(1)} %collective-permute-done.9.refs_1_, bf16[4,768]{1,0:T(4,128)(2,1)S(1)} %collective-permute-done.10.refs_2_, bf16[4,768]{1,0:T(4,128)(2,1)S(1)} %collective-permute-done.11.refs_3_), custom_call_target="tpu_custom_call" | custom-call | flops 1000000000 | bytes 1048576 | tf_op jit(solution)/shard_map/pallas_call | solution.py:178
  (9 shorter events, 0.0 us)
Async XLA Ops:
  0.6 0.7 %copy-start.5 = (s32[4]{0:T(128)S(1)}, s32[4]{0:T(128)}, u32[]{:S(2)}) copy-start(s32[4]{0:T(128)} %order_ref.1) | copy-start | bytes 52
  0.6 0.7 %copy-start.1 = (bf16[1,4,3072]{2,1,0:T(4,128)(2,1)S(1)}, bf16[1,4,3072]{2,1,0:T(4,128)(2,1)}, u32[]{:S(2)}) copy-start(bf16[1,4,3072]{2,1,0:T(4,128)(2,1)} %param.8) | copy-start | bytes 73732
  0.7 0.9 %copy-start.4 = (bf16[1,4,4,2,3072]{4,3,2,1,0:T(2,128)(2,1)S(1)}, bf16[1,4,4,2,3072]{4,3,2,1,0:T(2,128)(2,1)}, u32[]{:S(2)}) copy-start(bf16[1,4,4,2,3072]{4,3,2,1,0:T(2,128)(2,1)} %cache_ref.1) | copy-start | bytes 589828
  0.7 11.9 %copy-start.3 = (s32[4]{0:T(128)S(1)}, s32[4]{0:T(128)}, u32[]{:S(2)}) copy-start(s32[4]{0:T(128)} %step_ref.1) | copy-start | bytes 52
  0.7 11.9 %copy-start = (f32[1,4,3,3072]{3,1,2,0:T(4,128)S(1)}, f32[1,4,3,3072]{3,1,2,0:T(4,128)}, u32[]{:S(2)}) copy-start(f32[1,4,3,3072]{3,1,2,0:T(4,128)} %param.13) | copy-start | bytes 442372
  0.7 11.9 %copy-start.2 = (f32[1,2,128]{2,1,0:T(2,128)S(1)}, f32[1,2,128]{2,1,0:T(2,128)}, u32[]{:S(2)}) copy-start(f32[1,2,128]{2,1,0:T(2,128)} %param.12) | copy-start | bytes 3076
  0.7 11.9 %slice-start = ((s8[14155776]{0:T(1024)(128)(4,1)}), s8[4194304]{0:T(1024)(128)(4,1)S(1)}, s32[]{:S(2)}) async-start(s8[14155776]{0:T(1024)(128)(4,1)} %bitcast.9), calls=%async_computation | async-start | bytes 8388608
  0.7 11.9 %slice-start.1 = ((s8[14155776]{0:T(1024)(128)(4,1)}), s8[4194304]{0:T(1024)(128)(4,1)S(1)}, s32[]{:S(2)}) async-start(s8[14155776]{0:T(1024)(128)(4,1)} %bitcast.9), calls=%async_computation.1 | async-start | bytes 8388608
  1.6 11.0 %slice-start.2 = ((s8[14155776]{0:T(1024)(128)(4,1)}), s8[4194304]{0:T(1024)(128)(4,1)S(1)}, s32[]{:S(2)}) async-start(s8[14155776]{0:T(1024)(128)(4,1)} %bitcast.9), calls=%async_computation.2 | async-start | bytes 8388608
  1.6 11.0 %slice-start.3 = ((s8[14155776]{0:T(1024)(128)(4,1)}), s8[1572864]{0:T(1024)(128)(4,1)S(1)}, s32[]{:S(2)}) async-start(s8[14155776]{0:T(1024)(128)(4,1)} %bitcast.9), calls=%async_computation.3 | async-start | bytes 3145728
  2.3 20.4 %slice-start.4 = ((s8[4718592]{0:T(1024)(128)(4,1)}), s8[4194304]{0:T(1024)(128)(4,1)S(1)}, s32[]{:S(2)}) async-start(s8[4718592]{0:T(1024)(128)(4,1)} %bitcast.18), calls=%async_computation.4 | async-start | bytes 8388608
  2.3 10.3 %collective-permute-start = (bf16[40,768]{1,0:T(8,128)(2,1)S(1)}, bf16[40,768]{1,0:T(8,128)(2,1)S(1)}, u32[]{:S(2)}, u32[]{:S(2)}) collective-permute-start(bf16[40,768]{1,0:T(8,128)(2,1)S(1)} %get-tuple-element.21), channel_id=1, source_target_pairs={{0,12},{1,13},{2,14},{3,15},{4,8},{5,9},{6,10},{7,11},{8,4},{9,5},... | collective-permute-start | bytes 184328 | tf_op jit(solution)/shard_map/ppermute | solution.py:210
  7.4 5.1 %collective-permute-start.1 = (bf16[4,3072]{1,0:T(4,128)(2,1)S(1)}, bf16[4,3072]{1,0:T(4,128)(2,1)S(1)}, u32[]{:S(2)}, u32[]{:S(2)}) collective-permute-start(bf16[4,3072]{1,0:T(4,128)(2,1)S(1)} %bitcast.14), channel_id=1, source_target_pairs={{0,8},{1,9},{2,10},{3,11},{4,12},{5,13},{6,14},{7,15},{8,0},{9,1},... | collective-permute-start | bytes 73736 | tf_op jit(solution)/shard_map/ppermute | solution.py:210
  7.4 5.1 %collective-permute-start.2 = (bf16[4,3072]{1,0:T(4,128)(2,1)S(1)}, bf16[4,3072]{1,0:T(4,128)(2,1)S(1)}, u32[]{:S(2)}, u32[]{:S(2)}) collective-permute-start(bf16[4,3072]{1,0:T(4,128)(2,1)S(1)} %bitcast.15), channel_id=1, source_target_pairs={{0,4},{1,5},{2,6},{3,7},{4,0},{5,1},{6,2},{7,3},{8,12},{9,13},{10,... | collective-permute-start | bytes 73736 | tf_op jit(solution)/shard_map/ppermute | solution.py:210
  8.1 7.3 %collective-permute-start.3 = (bf16[24,768]{1,0:T(8,128)(2,1)S(1)}, bf16[24,768]{1,0:T(8,128)(2,1)S(1)}, u32[]{:S(2)}, u32[]{:S(2)}) collective-permute-start(bf16[24,768]{1,0:T(8,128)(2,1)S(1)} %get-tuple-element.29), channel_id=1, source_target_pairs={{0,8},{1,9},{2,10},{3,11},{4,12},{5,13},{6,14},{7,15},{8,0},{9,1},... | collective-permute-start | bytes 110600 | tf_op jit(solution)/shard_map/ppermute | solution.py:210
  10.4 5.0 %collective-permute-start.4 = (bf16[24,768]{1,0:T(8,128)(2,1)S(1)}, bf16[24,768]{1,0:T(8,128)(2,1)S(1)}, u32[]{:S(2)}, u32[]{:S(2)}) collective-permute-start(bf16[24,768]{1,0:T(8,128)(2,1)S(1)} %get-tuple-element.30), channel_id=1, source_target_pairs={{0,4},{1,5},{2,6},{3,7},{4,0},{5,1},{6,2},{7,3},{8,12},{9,13},{10,... | collective-permute-start | bytes 110600 | tf_op jit(solution)/shard_map/ppermute | solution.py:210
  12.6 10.0 %slice-start.5 = ((s8[4718592]{0:T(1024)(128)(4,1)}), s8[524288]{0:T(1024)(128)(4,1)S(1)}, s32[]{:S(2)}) async-start(s8[4718592]{0:T(1024)(128)(4,1)} %bitcast.18), calls=%async_computation.5 | async-start | bytes 1048576
  15.8 5.8 %collective-permute-start.5 = (bf16[24,768]{1,0:T(8,128)(2,1)S(1)}, bf16[24,768]{1,0:T(8,128)(2,1)S(1)}, u32[]{:S(2)}, u32[]{:S(2)}) collective-permute-start(bf16[24,768]{1,0:T(8,128)(2,1)S(1)} %get-tuple-element.32), channel_id=1, source_target_pairs={{0,12},{1,13},{2,14},{3,15},{4,8},{5,9},{6,10},{7,11},{8,4},{9,5},... | collective-permute-start | bytes 110600 | tf_op jit(solution)/shard_map/ppermute | solution.py:210
  17.4 5.3 %collective-permute-start.6 = (bf16[24,768]{1,0:T(8,128)(2,1)S(1)}, bf16[24,768]{1,0:T(8,128)(2,1)S(1)}, u32[]{:S(2)}, u32[]{:S(2)}) collective-permute-start(bf16[24,768]{1,0:T(8,128)(2,1)S(1)} %get-tuple-element.33), channel_id=1, source_target_pairs={{0,8},{1,9},{2,10},{3,11},{4,12},{5,13},{6,14},{7,15},{8,0},{9,1},... | collective-permute-start | bytes 110600 | tf_op jit(solution)/shard_map/ppermute | solution.py:210
  18.3 4.4 %collective-permute-start.7 = (bf16[24,768]{1,0:T(8,128)(2,1)S(1)}, bf16[24,768]{1,0:T(8,128)(2,1)S(1)}, u32[]{:S(2)}, u32[]{:S(2)}) collective-permute-start(bf16[24,768]{1,0:T(8,128)(2,1)S(1)} %get-tuple-element.34), channel_id=1, source_target_pairs={{0,4},{1,5},{2,6},{3,7},{4,0},{5,1},{6,2},{7,3},{8,12},{9,13},{10,... | collective-permute-start | bytes 110600 | tf_op jit(solution)/shard_map/ppermute | solution.py:210
  23.4 5.9 %collective-permute-start.8 = (bf16[4,768]{1,0:T(4,128)(2,1)S(1)}, bf16[4,768]{1,0:T(4,128)(2,1)S(1)}, u32[]{:S(2)}, u32[]{:S(2)}) collective-permute-start(bf16[4,768]{1,0:T(4,128)(2,1)S(1)} %get-tuple-element.36), channel_id=1, source_target_pairs={{0,13},{1,14},{2,15},{3,12},{4,9},{5,10},{6,11},{7,8},{8,5},{9,6},... | collective-permute-start | bytes 18440 | tf_op jit(solution)/shard_map/ppermute | solution.py:210
  23.5 5.8 %collective-permute-start.9 = (bf16[4,768]{1,0:T(4,128)(2,1)S(1)}, bf16[4,768]{1,0:T(4,128)(2,1)S(1)}, u32[]{:S(2)}, u32[]{:S(2)}) collective-permute-start(bf16[4,768]{1,0:T(4,128)(2,1)S(1)} %get-tuple-element.37), channel_id=1, source_target_pairs={{0,9},{1,10},{2,11},{3,8},{4,13},{5,14},{6,15},{7,12},{8,1},{9,2},... | collective-permute-start | bytes 18440 | tf_op jit(solution)/shard_map/ppermute | solution.py:210
  27.1 4.0 %collective-permute-start.10 = (bf16[4,768]{1,0:T(4,128)(2,1)S(1)}, bf16[4,768]{1,0:T(4,128)(2,1)S(1)}, u32[]{:S(2)}, u32[]{:S(2)}) collective-permute-start(bf16[4,768]{1,0:T(4,128)(2,1)S(1)} %get-tuple-element.38), channel_id=1, source_target_pairs={{0,5},{1,6},{2,7},{3,4},{4,1},{5,2},{6,3},{7,0},{8,13},{9,14},{10,... | collective-permute-start | bytes 18440 | tf_op jit(solution)/shard_map/ppermute | solution.py:210
  27.1 4.0 %collective-permute-start.11 = (bf16[4,768]{1,0:T(4,128)(2,1)S(1)}, bf16[4,768]{1,0:T(4,128)(2,1)S(1)}, u32[]{:S(2)}, u32[]{:S(2)}) collective-permute-start(bf16[4,768]{1,0:T(4,128)(2,1)S(1)} %get-tuple-element.39), channel_id=1, source_target_pairs={{0,1},{1,2},{2,3},{3,0},{4,5},{5,6},{6,7},{7,4},{8,9},{9,10},{10,1... | collective-permute-start | bytes 18440 | tf_op jit(solution)/shard_map/ppermute | solution.py:210

commit v2 on v1

--- a/solution.py
+++ b/solution.py
@@ -10,6 +10,7 @@
 
 
 APART = (1, 2)
+TURNS = ((3, 2), (0, 3), (2, 1), (1, 0))
 
 F32 = jnp.float32
 BF16 = jnp.bfloat16
@@ -87,11 +88,11 @@
         parts.append(dotted.astype(BF16).astype(F32))
     normed_heads = []
     for part in range(2):
-        gain = gain_ref[pl.ds(part, 1), :]
+        stacked = jnp.concatenate([parts[part][:, h * size : (h + 1) * size] for h in range(heads)], axis=0)
+        stacked = head_norm(stacked, gain_ref[pl.ds(part, 1), :])
+        length = slots * tokens
         normed_heads.append(
-            jnp.concatenate(
-                [head_norm(parts[part][:, h * size : (h + 1) * size], gain) for h in range(heads)], axis=1
-            )
+            jnp.concatenate([stacked[h * length : (h + 1) * length] for h in range(heads)], axis=1)
         )
     q_ref[...] = normed_heads[0].astype(BF16)
     keys, values = normed_heads[1], parts[2]
@@ -140,27 +141,39 @@
         outs[b][length:] = fresh_refs[b][...]
 
 
-def output_kernel(gate_ref, held_ref, weight_ref, *refs, slots, tokens):
+def partial_kernel(weight_ref, *refs, numbers, rows, before):
     columns = weight_ref.shape[1]
-    attention = refs[:slots][::-1]
     mine = lax.axis_index("seq")
-    total = None
-    for b in range(slots):
+    total = refs[len(numbers)][...] if before else None
+    for ref, b in zip(refs[: len(numbers)], numbers, strict=True):
         start = pl.multiple_of((mine ^ b) * columns, columns)
-        term = jnp.dot(attention[b][: slots * tokens], weight_ref[pl.ds(start, columns), :], preferred_element_type=F32)
+        term = jnp.dot(ref[:rows], weight_ref[pl.ds(start, columns), :], preferred_element_type=F32)
         total = term if total is None else total + term
+    refs[-1][...] = total
+
+
+def output_kernel(gate_ref, held_ref, weight_ref, total_ref, attention_ref, *outs, number, tokens, turns):
+    columns = weight_ref.shape[1]
+    start = pl.multiple_of((lax.axis_index("seq") ^ number) * columns, columns)
+    rows = total_ref.shape[0]
+    total = total_ref[...] + jnp.dot(
+        attention_ref[:rows], weight_ref[pl.ds(start, columns), :], preferred_element_type=F32
+    )
     block = held_ref[...].astype(F32) + gate_ref[...] * total.astype(BF16).astype(F32)
-    for b in range(slots):
-        refs[slots + b][...] = block[b * tokens : (b + 1) * tokens].astype(BF16)
-
-
-def place_kernel(*refs, slots):
+    pieces = [block[b * tokens : (b + 1) * tokens] for b in range(len(outs))]
+    even = lax.rem(lax.axis_index("section"), 2) == 0
+    for out, (b, c) in zip(outs, turns, strict=True):
+        out[...] = jnp.where(even, pieces[b], pieces[c]).astype(BF16)
+
+
+def place_kernel(*refs, slots, turns):
     out_ref, refs = refs[slots], refs[:slots][::-1]
     columns = refs[0].shape[1]
-    mine = lax.axis_index("seq")
-    for b in range(slots):
-        start = pl.multiple_of((mine ^ b) * columns, columns)
-        out_ref[0, :, pl.ds(start, columns)] = refs[b][...]
+    mine, sections = lax.axis_index("seq"), lax.axis_size("section")
+    even = lax.rem(lax.axis_index("section") + (sections - 1), sections) % 2 == 0
+    for ref, (b, c) in zip(refs, turns, strict=True):
+        start = pl.multiple_of((mine ^ jnp.where(even, b, c)) * columns, columns)
+        out_ref[0, :, pl.ds(start, columns)] = ref[...]
 
 
 def place_kv_kernel(*refs, slots, tokens):
@@ -197,13 +210,17 @@
     columns, size = w_qkv.shape[3], norm_gain.shape[2]
     heads, stale, rows = columns // size, (patches - 1) * tokens, slots * tokens
     split = apart(slots)
+    turns = TURNS if slots == 4 else [(b, b) for b in range(slots)]
 
     def array(*shape, dtype=BF16):
         return jax.ShapeDtypeStruct(shape, dtype)
 
-    def moved(array, number, onward=0):
+    def moved(array, number):
+        return lax.ppermute(array, "seq", [(j, j ^ number) for j in range(slots)])
+
+    def onward(array, turn):
         pairs = [
-            (j * sections + s, (j ^ number) * sections + (s + onward) % sections)
+            (j * sections + s, (j ^ turn[s % 2]) * sections + (s + 1) % sections)
             for j in range(slots)
             for s in range(sections)
         ]
@@ -260,18 +277,36 @@
         size=size,
     )
     attention = exchanged(ordered)
+    weights = w_out[0]
+    groups = [(0, slots - 1)] + [(b,) for b in range(slots - 2, 1, -1)] if slots > 2 else [(0,)]
+    total = []
+    for numbers in groups:
+        operands = [weights] + [attention[b] for b in numbers] + total
+        total = [
+            call(
+                partial_kernel,
+                1e9,
+                array(rows, columns, dtype=F32),
+                [],
+                operands,
+                numbers=numbers,
+                rows=rows,
+                before=bool(total),
+            )
+        ]
     pieces = call(
         output_kernel,
         2e9,
         [array(tokens, columns)] * slots,
         [],
-        [gate, held, w_out[0], *attention[::-1]],
-        slots=slots,
+        [gate, held, weights, *total, attention[1]],
+        number=1,
         tokens=tokens,
-    )
-    arrived = [moved(pieces[b], b, onward=1) for b in range(slots)]
+        turns=turns,
+    )
+    arrived = [onward(piece, turn) for piece, turn in zip(pieces, turns, strict=True)]
     fresh_kv = call(place_kv_kernel, 1e9, array(1, tokens, 2, width), [], attention[::-1], slots=slots, tokens=tokens)
-    next_hidden = call(place_kernel, 1e9, array(1, tokens, width), [], arrived[::-1], slots=slots)
+    next_hidden = call(place_kernel, 1e9, array(1, tokens, width), [], arrived[::-1], slots=slots, turns=turns)
     return (next_hidden, fresh_kv)
 
 

time: 31.9 us -> 33.3 us (1.044)
  the two profiles are of different devices: /device:TPU:0 before, /device:TPU:1 now
where the time goes in v2:
time: 33.3 us; the launch traced here: 33.2 us
  starting transfers between devices  19.5 us (59%)
  Pallas kernels  6.09 us (18%)
  waiting for transfers between devices  5.84 us (18%)
  local copies, waits for them, and re-layouts  0.92 us (3%)
  between operations  0.84 us (3%)
    ppermute x8, starting transfers between devices, moved(): return lax.ppermute(array, 'seq', [(j, j ^ number) for j in range(slots)])  11.6 us
    ppermute x4, starting transfers between devices, onward(): return lax.ppermute(array, ('seq', 'section'), pairs)  7.84 us
    pallas_call x9, Pallas kernels, call(): pl.pallas_call(functools.partial(kernel, **sizes), out_shape=out_shape, i...  6.09 us
    ppermute x4, waiting for transfers between devices, onward(): return lax.ppermute(array, ('seq', 'section'), pairs)  4.14 us
    ppermute x8, waiting for transfers between devices, moved(): return lax.ppermute(array, 'seq', [(j, j ^ number) for j in range(slots)])  1.7 us
    unnamed x24, local copies, waits for them, and re-layouts  0.92 us
  transfers between devices with their start and end apart: 12, of which 4 were waited for; matrix products, arithmetic and copies ran while one was open for 0% of the time, Pallas kernels for 12%

profile of v2, /device:TPU:1, one launch (start us, length us, event | category | flops | bytes accessed | tf_op | source)
XLA Modules:
  0.0 33.2 jit_solution(5476103723846650948)
XLA Ops:
  0.6 0.0 copy-start.5
  0.7 0.0 slice-start.2
  0.7 0.0 slice-start.3
  0.7 0.6 %copy-done.5 = s32[4]{0:T(128)S(1)} copy-done((s32[4]{0:T(128)S(1)}, s32[4]{0:T(128)}, u32[]{:S(2)}) %copy-start.5) | copy-done | bytes 40
  1.3 0.1 copy-done.1
  1.4 0.2 copy-done.4
  1.6 0.7 %shard_map.96 = (bf16[24,768]{1,0:T(8,128)(2,1)S(1)}, bf16[24,768]{1,0:T(8,128)(2,1)S(1)}, bf16[24,768]{1,0:T(8,128)(2,1)S(1)}, bf16[40,768]{1,0:T(8,128)(2,1)S(1)}) custom-call(s32[4]{0:T(128)S(1)} %copy-done.5, f32[8,128]{1,0:T(8,128)S(1)} %shard_map.95._, bf16[4,3072]{1,0:T(4,128)(2,1)S(1)} %bitcast.18, bf16[1,4,4,2,3072]{4,3,2,1,0:T(2,128)(2,1)S(1)} %copy-done.4), custom_call_target="tpu_custom_call" | custom-call | flops 5000000000 | bytes 1048576 | tf_op jit(solution)/shard_map/pallas_call | solution.py:191
  2.3 0.0 slice-start
  2.3 4.2 %collective-permute-start = (bf16[40,768]{1,0:T(8,128)(2,1)S(1)}, bf16[40,768]{1,0:T(8,128)(2,1)S(1)}, u32[]{:S(2)}, u32[]{:S(2)}) collective-permute-start(bf16[40,768]{1,0:T(8,128)(2,1)S(1)} %get-tuple-element.21), channel_id=1, source_target_pairs={{0,12},{4,8},{8,4},{12,0},{1,13},{5,9},{9,5},{13,1},{2,14},{6,10},... | collective-permute-start | bytes 184328 | tf_op jit(solution)/shard_map/ppermute | solution.py:219
  6.5 0.0 collective-permute-start.1
  6.5 0.4 %collective-permute-start.2 = (bf16[4,3072]{1,0:T(4,128)(2,1)S(1)}, bf16[4,3072]{1,0:T(4,128)(2,1)S(1)}, u32[]{:S(2)}, u32[]{:S(2)}) collective-permute-start(bf16[4,3072]{1,0:T(4,128)(2,1)S(1)} %bitcast.20), channel_id=1, source_target_pairs={{0,4},{4,0},{8,12},{12,8},{1,5},{5,1},{9,13},{13,9},{2,6},{6,2},{1... | collective-permute-start | bytes 73736 | tf_op jit(solution)/shard_map/ppermute | solution.py:219
  6.9 2.0 %collective-permute-start.3 = (bf16[24,768]{1,0:T(8,128)(2,1)S(1)}, bf16[24,768]{1,0:T(8,128)(2,1)S(1)}, u32[]{:S(2)}, u32[]{:S(2)}) collective-permute-start(bf16[24,768]{1,0:T(8,128)(2,1)S(1)} %get-tuple-element.29), channel_id=1, source_target_pairs={{0,8},{4,12},{8,0},{12,4},{1,9},{5,13},{9,1},{13,5},{2,10},{6,14},... | collective-permute-start | bytes 110600 | tf_op jit(solution)/shard_map/ppermute | solution.py:219
  8.9 1.5 %collective-permute-start.4 = (bf16[24,768]{1,0:T(8,128)(2,1)S(1)}, bf16[24,768]{1,0:T(8,128)(2,1)S(1)}, u32[]{:S(2)}, u32[]{:S(2)}) collective-permute-start(bf16[24,768]{1,0:T(8,128)(2,1)S(1)} %get-tuple-element.30), channel_id=1, source_target_pairs={{0,4},{4,0},{8,12},{12,8},{1,5},{5,1},{9,13},{13,9},{2,6},{6,2},{1... | collective-permute-start | bytes 110600 | tf_op jit(solution)/shard_map/ppermute | solution.py:219
  10.3 0.0 collective-permute-done.1.refs_1_
  10.3 0.0 collective-permute-done.2.refs_2_
  10.3 0.0 collective-permute-done.refs_0_.refs_4_
  10.3 0.0 copy-done.3
  10.4 0.0 copy-done
  10.4 0.0 copy-done.2
  10.4 0.0 slice-done.2
  10.4 0.0 slice-done.3
  10.4 0.0 slice-done.4
  10.4 0.0 slice-done.5
  10.4 0.0 slice-start.1
  10.4 2.7 %shard_map.97 = (bf16[16,768]{1,0:T(8,128)(2,1)S(1)}, bf16[16,768]{1,0:T(8,128)(2,1)S(1)}, f32[1,768]{1,0:T(1,128)S(1)}, bf16[8,768]{1,0:T(8,128)(2,1)S(1)}, bf1...) custom-call(s32[4]{0:T(128)S(1)} %copy-done.3, f32[3,4,3072]{2,1,0:T(4,128)S(1)} %bitcast.17, ...), custom_call_target="tpu_custom_call" | custom-call | flops 2000000000 | bytes 1048576 | tf_op jit(solution)/shard_map/pallas_call | solution.py:191
  13.1 0.0 collective-permute-done.3.refs_5_
  13.1 0.0 collective-permute-done.4.refs_6_
  13.1 0.4 %shard_map.98 = (bf16[24,768]{1,0:T(8,128)(2,1)S(1)}, bf16[24,768]{1,0:T(8,128)(2,1)S(1)}, bf16[24,768]{1,0:T(8,128)(2,1)S(1)}, bf16[24,768]{1,0:T(8,128)(2,1)S(1)}) custom-call(bf16[16,768]{1,0:T(8,128)(2,1)S(1)} %get-tuple-element.24.q_ref, bf16[8,768]{1,0:T(8,128)(2,1)S(1)} %get-tuple-element.25.refs_0_, bf16[8,768]{1,0:T(8,128)(2,1)S(1)} %get-tuple-element.26.refs_1_, ...), custom_call_target="tpu_custom_call" | custom-call | flops 2000000000 | bytes 1048576 | tf_op jit(solution)/shard_map/pallas_call | solution.py:191
  13.6 1.7 %collective-permute-start.6 = (bf16[24,768]{1,0:T(8,128)(2,1)S(1)}, bf16[24,768]{1,0:T(8,128)(2,1)S(1)}, u32[]{:S(2)}, u32[]{:S(2)}) collective-permute-start(bf16[24,768]{1,0:T(8,128)(2,1)S(1)} %get-tuple-element.34), channel_id=1, source_target_pairs={{0,12},{4,8},{8,4},{12,0},{1,13},{5,9},{9,5},{13,1},{2,14},{6,10},... | collective-permute-start | bytes 110600 | tf_op jit(solution)/shard_map/ppermute | solution.py:219
  15.3 0.0 collective-permute-start.5
  15.3 1.9 %collective-permute-start.7 = (bf16[24,768]{1,0:T(8,128)(2,1)S(1)}, bf16[24,768]{1,0:T(8,128)(2,1)S(1)}, u32[]{:S(2)}, u32[]{:S(2)}) collective-permute-start(bf16[24,768]{1,0:T(8,128)(2,1)S(1)} %get-tuple-element.35), channel_id=1, source_target_pairs={{0,4},{4,0},{8,12},{12,8},{1,5},{5,1},{9,13},{13,9},{2,6},{6,2},{1... | collective-permute-start | bytes 110600 | tf_op jit(solution)/shard_map/ppermute | solution.py:219
  17.2 1.1 %collective-permute-done.6.refs_1_.refs_0_ = bf16[24,768]{1,0:T(8,128)(2,1)S(1)} collective-permute-done((bf16[24,768]{1,0:T(8,128)(2,1)S(1)}, bf16[24,768]{1,0:T(8,128)(2,1)S(1)}, u32[]{:S(2)}, u32[]{:S(2)}) %collective-permute-start.6) | collective-permute-done | bytes 36896 | tf_op jit(solution)/shard_map/ppermute | solution.py:219
  18.2 0.0 slice-done.1
  18.3 0.4 %shard_map.99.refs_1_ = f32[16,768]{1,0:T(8,128)S(1)} custom-call(bf16[3072,768]{1,0:T(8,128)(2,1)S(1)} %bitcast.11, bf16[24,768]{1,0:T(8,128)(2,1)S(1)} %get-tuple-element.33.refs_0_.refs_3_, bf16[24,768]{1,0:T(8,128)(2,1)S(1)} %collective-permute-done.6.refs_1_.refs_0_), custom_call_target="tpu_custom_call" | custom-call | flops 1000000000 | bytes 1048576 | tf_op jit(solution)/shard_map/pallas_call | solution.py:191
  18.7 0.6 %collective-permute-done.5.refs_0_.refs_1_ = bf16[24,768]{1,0:T(8,128)(2,1)S(1)} collective-permute-done((bf16[24,768]{1,0:T(8,128)(2,1)S(1)}, bf16[24,768]{1,0:T(8,128)(2,1)S(1)}, u32[]{:S(2)}, u32[]{:S(2)}) %collective-permute-start.5) | collective-permute-done | bytes 36896 | tf_op jit(solution)/shard_map/ppermute | solution.py:219
  19.3 0.3 shard_map.100.total_ref
  19.6 0.0 collective-permute-done.7.attention_ref.refs_2_
  19.6 0.3 shard_map.101
  19.9 4.5 %collective-permute-start.8 = (bf16[4,768]{1,0:T(4,128)(2,1)S(1)}, bf16[4,768]{1,0:T(4,128)(2,1)S(1)}, u32[]{:S(2)}, u32[]{:S(2)}) collective-permute-start(bf16[4,768]{1,0:T(4,128)(2,1)S(1)} %get-tuple-element.36), channel_id=1, source_target_pairs={{0,5},{1,2},{2,7},{3,0},{4,1},{5,6},{6,3},{7,4},{8,13},{9,10},{10,... | collective-permute-start | bytes 18440 | tf_op jit(solution)/shard_map/ppermute | solution.py:227
  24.4 0.7 %collective-permute-start.9 = (bf16[4,768]{1,0:T(4,128)(2,1)S(1)}, bf16[4,768]{1,0:T(4,128)(2,1)S(1)}, u32[]{:S(2)}, u32[]{:S(2)}) collective-permute-start(bf16[4,768]{1,0:T(4,128)(2,1)S(1)} %get-tuple-element.37), channel_id=1, source_target_pairs={{0,9},{1,6},{2,11},{3,4},{4,13},{5,2},{6,15},{7,0},{8,1},{9,14},{1... | collective-permute-start | bytes 18440 | tf_op jit(solution)/shard_map/ppermute | solution.py:227
  25.2 2.6 %collective-permute-start.10 = (bf16[4,768]{1,0:T(4,128)(2,1)S(1)}, bf16[4,768]{1,0:T(4,128)(2,1)S(1)}, u32[]{:S(2)}, u32[]{:S(2)}) collective-permute-start(bf16[4,768]{1,0:T(4,128)(2,1)S(1)} %get-tuple-element.38), channel_id=1, source_target_pairs={{0,1},{1,14},{2,3},{3,12},{4,5},{5,10},{6,7},{7,8},{8,9},{9,6},{10... | collective-permute-start | bytes 18440 | tf_op jit(solution)/shard_map/ppermute | solution.py:227
  27.7 0.0 collective-permute-start.11
  27.7 0.7 %shard_map.103 = bf16[1,4,2,3072]{3,2,1,0:T(2,128)(2,1)} custom-call(bf16[24,768]{1,0:T(8,128)(2,1)S(1)} %collective-permute-done.6.refs_1_.refs_0_, bf16[24,768]{1,0:T(8,128)(2,1)S(1)} %collective-permute-done.5.refs_0_.refs_1_, bf16[24,768]{1,0:T(8,128)(2,1)S(1)} %collective-permute-done.7.attention_ref.refs_2_, ...), custom_call_target="tpu_custom_call" | custom-call | flops 1000000000 | bytes 1048576 | tf_op jit(solution)/shard_map/pallas_call | solution.py:191
  28.4 0.0 collective-permute-done.8.refs_0_
  28.4 0.0 collective-permute-done.9.refs_1_
  28.4 0.1 collective-permute-done.10.refs_2_
  28.5 4.1 %collective-permute-done.11.refs_3_ = bf16[4,768]{1,0:T(4,128)(2,1)S(1)} collective-permute-done((bf16[4,768]{1,0:T(4,128)(2,1)S(1)}, bf16[4,768]{1,0:T(4,128)(2,1)S(1)}, u32[]{:S(2)}, u32[]{:S(2)}) %collective-permute-start.11) | collective-permute-done | bytes 6176 | tf_op jit(solution)/shard_map/ppermute | solution.py:227
  32.6 0.6 %shard_map.102 = bf16[1,4,3072]{2,1,0:T(4,128)(2,1)} custom-call(bf16[4,768]{1,0:T(4,128)(2,1)S(1)} %collective-permute-done.8.refs_0_, bf16[4,768]{1,0:T(4,128)(2,1)S(1)} %collective-permute-done.9.refs_1_, bf16[4,768]{1,0:T(4,128)(2,1)S(1)} %collective-permute-done.10.refs_2_, bf16[4,768]{1,0:T(4,128)(2,1)S(1)} %collective-permute-done.11.refs_3_), custom_call_target="tpu_custom_call" | custom-call | flops 1000000000 | bytes 1048576 | tf_op jit(solution)/shard_map/pallas_call | solution.py:191
  (11 shorter events, 0.0 us)
Async XLA Ops:
  0.6 0.7 %copy-start.5 = (s32[4]{0:T(128)S(1)}, s32[4]{0:T(128)}, u32[]{:S(2)}) copy-start(s32[4]{0:T(128)} %order_ref.1) | copy-start | bytes 52
  0.6 0.7 %copy-start.1 = (bf16[1,4,3072]{2,1,0:T(4,128)(2,1)S(1)}, bf16[1,4,3072]{2,1,0:T(4,128)(2,1)}, u32[]{:S(2)}) copy-start(bf16[1,4,3072]{2,1,0:T(4,128)(2,1)} %param.8) | copy-start | bytes 73732
  0.7 0.9 %copy-start.4 = (bf16[1,4,4,2,3072]{4,3,2,1,0:T(2,128)(2,1)S(1)}, bf16[1,4,4,2,3072]{4,3,2,1,0:T(2,128)(2,1)}, u32[]{:S(2)}) copy-start(bf16[1,4,4,2,3072]{4,3,2,1,0:T(2,128)(2,1)} %cache_ref.1) | copy-start | bytes 589828
  0.7 9.7 %copy-start.3 = (s32[4]{0:T(128)S(1)}, s32[4]{0:T(128)}, u32[]{:S(2)}) copy-start(s32[4]{0:T(128)} %step_ref.1) | copy-start | bytes 52
  0.7 9.7 %copy-start = (f32[1,4,3,3072]{3,1,2,0:T(4,128)S(1)}, f32[1,4,3,3072]{3,1,2,0:T(4,128)}, u32[]{:S(2)}) copy-start(f32[1,4,3,3072]{3,1,2,0:T(4,128)} %param.13) | copy-start | bytes 442372
  0.7 9.7 %copy-start.2 = (f32[1,2,128]{2,1,0:T(2,128)S(1)}, f32[1,2,128]{2,1,0:T(2,128)}, u32[]{:S(2)}) copy-start(f32[1,2,128]{2,1,0:T(2,128)} %param.12) | copy-start | bytes 3076
  0.7 9.7 %slice-start.2 = ((s8[14155776]{0:T(1024)(128)(4,1)}), s8[4194304]{0:T(1024)(128)(4,1)S(1)}, s32[]{:S(2)}) async-start(s8[14155776]{0:T(1024)(128)(4,1)} %bitcast.14), calls=%async_computation.2 | async-start | bytes 8388608
  0.7 9.7 %slice-start.3 = ((s8[14155776]{0:T(1024)(128)(4,1)}), s8[4194304]{0:T(1024)(128)(4,1)S(1)}, s32[]{:S(2)}) async-start(s8[14155776]{0:T(1024)(128)(4,1)} %bitcast.14), calls=%async_computation.3 | async-start | bytes 8388608
  1.6 8.8 %slice-start.4 = ((s8[14155776]{0:T(1024)(128)(4,1)}), s8[4194304]{0:T(1024)(128)(4,1)S(1)}, s32[]{:S(2)}) async-start(s8[14155776]{0:T(1024)(128)(4,1)} %bitcast.14), calls=%async_computation.4 | async-start | bytes 8388608
  1.6 8.8 %slice-start.5 = ((s8[14155776]{0:T(1024)(128)(4,1)}), s8[1572864]{0:T(1024)(128)(4,1)S(1)}, s32[]{:S(2)}) async-start(s8[14155776]{0:T(1024)(128)(4,1)} %bitcast.14), calls=%async_computation.5 | async-start | bytes 3145728
  2.3 16.0 %slice-start = ((s8[4718592]{0:T(1024)(128)(4,1)}), s8[4194304]{0:T(1024)(128)(4,1)S(1)}, s32[]{:S(2)}) async-start(s8[4718592]{0:T(1024)(128)(4,1)} %bitcast.9), calls=%async_computation | async-start | bytes 8388608
  2.3 8.0 %collective-permute-start = (bf16[40,768]{1,0:T(8,128)(2,1)S(1)}, bf16[40,768]{1,0:T(8,128)(2,1)S(1)}, u32[]{:S(2)}, u32[]{:S(2)}) collective-permute-start(bf16[40,768]{1,0:T(8,128)(2,1)S(1)} %get-tuple-element.21), channel_id=1, source_target_pairs={{0,12},{4,8},{8,4},{12,0},{1,13},{5,9},{9,5},{13,1},{2,14},{6,10},... | collective-permute-start | bytes 184328 | tf_op jit(solution)/shard_map/ppermute | solution.py:219
  6.5 3.8 %collective-permute-start.1 = (bf16[4,3072]{1,0:T(4,128)(2,1)S(1)}, bf16[4,3072]{1,0:T(4,128)(2,1)S(1)}, u32[]{:S(2)}, u32[]{:S(2)}) collective-permute-start(bf16[4,3072]{1,0:T(4,128)(2,1)S(1)} %bitcast.19), channel_id=1, source_target_pairs={{0,8},{4,12},{8,0},{12,4},{1,9},{5,13},{9,1},{13,5},{2,10},{6,14},... | collective-permute-start | bytes 73736 | tf_op jit(solution)/shard_map/ppermute | solution.py:219
  6.5 3.8 %collective-permute-start.2 = (bf16[4,3072]{1,0:T(4,128)(2,1)S(1)}, bf16[4,3072]{1,0:T(4,128)(2,1)S(1)}, u32[]{:S(2)}, u32[]{:S(2)}) collective-permute-start(bf16[4,3072]{1,0:T(4,128)(2,1)S(1)} %bitcast.20), channel_id=1, source_target_pairs={{0,4},{4,0},{8,12},{12,8},{1,5},{5,1},{9,13},{13,9},{2,6},{6,2},{1... | collective-permute-start | bytes 73736 | tf_op jit(solution)/shard_map/ppermute | solution.py:219
  6.9 6.3 %collective-permute-start.3 = (bf16[24,768]{1,0:T(8,128)(2,1)S(1)}, bf16[24,768]{1,0:T(8,128)(2,1)S(1)}, u32[]{:S(2)}, u32[]{:S(2)}) collective-permute-start(bf16[24,768]{1,0:T(8,128)(2,1)S(1)} %get-tuple-element.29), channel_id=1, source_target_pairs={{0,8},{4,12},{8,0},{12,4},{1,9},{5,13},{9,1},{13,5},{2,10},{6,14},... | collective-permute-start | bytes 110600 | tf_op jit(solution)/shard_map/ppermute | solution.py:219
  8.9 4.3 %collective-permute-start.4 = (bf16[24,768]{1,0:T(8,128)(2,1)S(1)}, bf16[24,768]{1,0:T(8,128)(2,1)S(1)}, u32[]{:S(2)}, u32[]{:S(2)}) collective-permute-start(bf16[24,768]{1,0:T(8,128)(2,1)S(1)} %get-tuple-element.30), channel_id=1, source_target_pairs={{0,4},{4,0},{8,12},{12,8},{1,5},{5,1},{9,13},{13,9},{2,6},{6,2},{1... | collective-permute-start | bytes 110600 | tf_op jit(solution)/shard_map/ppermute | solution.py:219
  10.4 7.8 %slice-start.1 = ((s8[4718592]{0:T(1024)(128)(4,1)}), s8[524288]{0:T(1024)(128)(4,1)S(1)}, s32[]{:S(2)}) async-start(s8[4718592]{0:T(1024)(128)(4,1)} %bitcast.9), calls=%async_computation.1 | async-start | bytes 1048576
  13.6 4.7 %collective-permute-start.6 = (bf16[24,768]{1,0:T(8,128)(2,1)S(1)}, bf16[24,768]{1,0:T(8,128)(2,1)S(1)}, u32[]{:S(2)}, u32[]{:S(2)}) collective-permute-start(bf16[24,768]{1,0:T(8,128)(2,1)S(1)} %get-tuple-element.34), channel_id=1, source_target_pairs={{0,12},{4,8},{8,4},{12,0},{1,13},{5,9},{9,5},{13,1},{2,14},{6,10},... | collective-permute-start | bytes 110600 | tf_op jit(solution)/shard_map/ppermute | solution.py:219
  15.3 4.0 %collective-permute-start.5 = (bf16[24,768]{1,0:T(8,128)(2,1)S(1)}, bf16[24,768]{1,0:T(8,128)(2,1)S(1)}, u32[]{:S(2)}, u32[]{:S(2)}) collective-permute-start(bf16[24,768]{1,0:T(8,128)(2,1)S(1)} %get-tuple-element.32), channel_id=1, source_target_pairs={{0,8},{4,12},{8,0},{12,4},{1,9},{5,13},{9,1},{13,5},{2,10},{6,14},... | collective-permute-start | bytes 110600 | tf_op jit(solution)/shard_map/ppermute | solution.py:219
  15.3 4.2 %collective-permute-start.7 = (bf16[24,768]{1,0:T(8,128)(2,1)S(1)}, bf16[24,768]{1,0:T(8,128)(2,1)S(1)}, u32[]{:S(2)}, u32[]{:S(2)}) collective-permute-start(bf16[24,768]{1,0:T(8,128)(2,1)S(1)} %get-tuple-element.35), channel_id=1, source_target_pairs={{0,4},{4,0},{8,12},{12,8},{1,5},{5,1},{9,13},{13,9},{2,6},{6,2},{1... | collective-permute-start | bytes 110600 | tf_op jit(solution)/shard_map/ppermute | solution.py:219
  19.9 8.6 %collective-permute-start.8 = (bf16[4,768]{1,0:T(4,128)(2,1)S(1)}, bf16[4,768]{1,0:T(4,128)(2,1)S(1)}, u32[]{:S(2)}, u32[]{:S(2)}) collective-permute-start(bf16[4,768]{1,0:T(4,128)(2,1)S(1)} %get-tuple-element.36), channel_id=1, source_target_pairs={{0,5},{1,2},{2,7},{3,0},{4,1},{5,6},{6,3},{7,4},{8,13},{9,10},{10,... | collective-permute-start | bytes 18440 | tf_op jit(solution)/shard_map/ppermute | solution.py:227
  24.4 4.0 %collective-permute-start.9 = (bf16[4,768]{1,0:T(4,128)(2,1)S(1)}, bf16[4,768]{1,0:T(4,128)(2,1)S(1)}, u32[]{:S(2)}, u32[]{:S(2)}) collective-permute-start(bf16[4,768]{1,0:T(4,128)(2,1)S(1)} %get-tuple-element.37), channel_id=1, source_target_pairs={{0,9},{1,6},{2,11},{3,4},{4,13},{5,2},{6,15},{7,0},{8,1},{9,14},{1... | collective-permute-start | bytes 18440 | tf_op jit(solution)/shard_map/ppermute | solution.py:227
  25.2 3.3 %collective-permute-start.10 = (bf16[4,768]{1,0:T(4,128)(2,1)S(1)}, bf16[4,768]{1,0:T(4,128)(2,1)S(1)}, u32[]{:S(2)}, u32[]{:S(2)}) collective-permute-start(bf16[4,768]{1,0:T(4,128)(2,1)S(1)} %get-tuple-element.38), channel_id=1, source_target_pairs={{0,1},{1,14},{2,3},{3,12},{4,5},{5,10},{6,7},{7,8},{8,9},{9,6},{10... | collective-permute-start | bytes 18440 | tf_op jit(solution)/shard_map/ppermute | solution.py:227
  27.7 4.9 %collective-permute-start.11 = (bf16[4,768]{1,0:T(4,128)(2,1)S(1)}, bf16[4,768]{1,0:T(4,128)(2,1)S(1)}, u32[]{:S(2)}, u32[]{:S(2)}) collective-permute-start(bf16[4,768]{1,0:T(4,128)(2,1)S(1)} %get-tuple-element.39), channel_id=1, source_target_pairs={{0,13},{1,10},{2,15},{3,8},{4,9},{5,14},{6,11},{7,12},{8,5},{9,2},... | collective-permute-start | bytes 18440 | tf_op jit(solution)/shard_map/ppermute | solution.py:227
